TPU v7x, 128 devices: a whole 4x4x4 slice. The times are simulated.
128 devices in a mesh: row: 8 (over y_hi, x), col: 16 (over z, y_lo, core).
Axes of the slice: x: 4, y: 4 (y_hi: 2, y_lo: 2; y = y_hi * 2 + y_lo), z: 4, core: 2. Of those that a mesh axis runs over, the one named last changes fastest.
Arguments:
- features: bfloat16 [64, 1024, 1024], P(None, 'col', 'row'), may hold values from -120 to 120
- conv_first: bfloat16 [9, 64, 64], replicated, may hold values from -0.25 to 0.25
- conv_second: bfloat16 [9, 64, 64], replicated, may hold values from -0.25 to 0.25
- head_weight: bfloat16 [37, 64], replicated, may hold values from -0.75 to 0.75
- head_bias: float32 [37], replicated, may hold values from -4 to 4
- cotangent: bfloat16 [37, 1024, 1024], P(None, 'col', 'row'), may hold values from -6 to 6
Outputs:
- logits: bfloat16 [37, 1024, 1024], P(None, 'col', 'row')
- input_grad: bfloat16 [64, 1024, 1024], P(None, 'col', 'row')
- grad_first: float32 [9, 64, 64], replicated
- grad_second: float32 [9, 64, 64], replicated
- grad_head: float32 [37, 64], replicated
- grad_bias: float32 [37], replicated
All inputs are finite; a program needn't handle non-finite values.
Results may differ from a plain program's by a relative error of at most 0.007.
Values may be sent and summed in bfloat16 or wider, within the bound.
No kernel may reach another device: no remote copies, remote signals or barrier semaphores. Data moves between devices by JAX's collectives and lax.ppermute only.
A program may use at most 128 MiB of HBM per device.

v0:
```python
import jax
import jax.numpy as jnp
from jax import lax
from jax.sharding import PartitionSpec as P

DILATION_STEP = 16
epsilon = 1e-05


def with_halo(block, sides, width):
    for axis, dim in sides:
        count = lax.axis_size(axis)
        forward = [(i, i + 1) for i in range(count - 1)]
        backward = [(target, source) for source, target in forward]
        low = lax.ppermute(
            lax.slice_in_dim(block, block.shape[dim] - width, None, axis=dim), axis, forward
        )
        high = lax.ppermute(lax.slice_in_dim(block, 0, width, axis=dim), axis, backward)
        block = jnp.concatenate([low, block, high], axis=dim)
    return block


def as_sent(shard):

    def short(part):
        return part.astype(jnp.bfloat16) if part.dtype == jnp.float32 else part

    return jax.tree.map(short, shard)


def elu_apply(value_entries):
    return jnp.where(
        value_entries > 0, value_entries, jnp.exp(jnp.minimum(value_entries, 0.0)) - 1.0
    )


def elu_slope(value_entries):
    return jnp.where(value_entries > 0, 1.0, jnp.exp(jnp.minimum(value_entries, 0.0)))


def widen(value_entries):
    return with_halo(value_entries, (("row", 2), ("col", 1)), DILATION_STEP)


def widen_grad(value_entries):
    return with_halo(value_entries, (("row", 2), ("col", 1)), DILATION_STEP)


def tap_window(padded, kernel_row, kernel_column, adjoint, col_count, row_count):
    shift_direction = -1 if adjoint else 1
    column_shift = DILATION_STEP + shift_direction * DILATION_STEP * (kernel_column - 1)
    row_shift = DILATION_STEP + shift_direction * DILATION_STEP * (kernel_row - 1)
    window = padded[:, column_shift : column_shift + col_count, row_shift : row_shift + row_count]
    return window.reshape(padded.shape[0], col_count * row_count)


def convolve(padded, weights, col_count, row_count, adjoint):
    running = jnp.zeros((weights.shape[1], col_count * row_count), jnp.float32)
    for kernel_row in range(3):
        for kernel_column in range(3):
            window = tap_window(padded, kernel_row, kernel_column, adjoint, col_count, row_count)
            matrix = weights[3 * kernel_row + kernel_column]
            if adjoint:
                matrix = matrix.T
            running = running + jnp.dot(matrix, window, preferred_element_type=jnp.float32)
    return running.reshape(-1, col_count, row_count)


def weight_terms(gradient, padded, col_count, row_count):
    flattened = gradient.reshape(gradient.shape[0], -1)
    collected = []
    for kernel_row in range(3):
        for kernel_column in range(3):
            window = tap_window(padded, kernel_row, kernel_column, False, col_count, row_count)
            collected.append(
                lax.dot_general(
                    flattened, window, (((1,), (1,)), ((), ())), preferred_element_type=jnp.float32
                )
            )
    return jnp.stack(collected, 0)


def normalize(activation, cell_count):
    totals = lax.psum(jnp.sum(activation, axis=(1, 2)), ("row", "col"))
    average = totals / cell_count
    centered = activation - average[:, None, None]
    spread = lax.psum(jnp.sum(centered * centered, axis=(1, 2)), ("row", "col")) / cell_count
    inverse_std = lax.rsqrt(spread + epsilon)
    return (centered * inverse_std[:, None, None], inverse_std)


def norm_back(gradient, normed, inverse_std, cell_count):
    first_sum, second_sum = lax.psum(
        (jnp.sum(gradient, axis=(1, 2)), jnp.sum(gradient * normed, axis=(1, 2))), ("row", "col")
    )
    first_mean = first_sum / cell_count
    second_mean = second_sum / cell_count
    return inverse_std[:, None, None] * (
        gradient - first_mean[:, None, None] - normed * second_mean[:, None, None]
    )


def mirror_prepare(tensor, col_devices):
    planes, col_count, row_count = tensor.shape
    slab_rows = row_count // col_devices
    shaped = tensor.reshape(planes, col_count, col_devices, slab_rows).transpose(2, 1, 0, 3)
    return shaped.reshape(col_devices, col_count, planes * slab_rows)


def mirror_middle(received):
    return received.reshape(received.shape[1], 1, received.shape[2])


def mirror_tail(received, col_devices, row_devices):
    return received.reshape(received.shape[0], col_devices, row_devices, received.shape[2])


def mirror_finish(received, planes, row_devices):
    row_count = received.shape[0]
    slab_rows = received.shape[3] // planes
    shaped = received.reshape(row_count, row_devices, planes, slab_rows).transpose(2, 1, 3, 0)
    return shaped.reshape(planes, row_devices * slab_rows, row_count)


def mirror_half(tensors):
    col_devices = lax.axis_size("col")
    row_devices = lax.axis_size("row")
    planes = tuple((member.shape[0] for member in tensors))
    first = lax.all_to_all(
        as_sent(tuple((mirror_prepare(member, col_devices) for member in tensors))),
        "col",
        split_axis=0,
        concat_axis=1,
        tiled=True,
    )
    second = lax.all_to_all(
        as_sent(tuple((mirror_middle(member) for member in first))),
        ("row", "col"),
        split_axis=0,
        concat_axis=1,
        tiled=True,
    )
    third = lax.all_to_all(
        as_sent(tuple((mirror_tail(member, col_devices, row_devices) for member in second))),
        "col",
        split_axis=1,
        concat_axis=0,
        tiled=True,
    )
    return tuple(
        (
            mirror_finish(member, count_planes, row_devices)
            for member, count_planes in zip(third, planes)
        )
    )


def mirror_full(tensors):
    col_devices = lax.axis_size("col")
    row_devices = lax.axis_size("row")
    planes = tuple((member.shape[0] for member in tensors))
    first = lax.all_to_all(
        tuple((mirror_prepare(member, col_devices) for member in tensors)),
        "col",
        split_axis=0,
        concat_axis=1,
        tiled=True,
    )
    second = lax.all_to_all(
        tuple((mirror_middle(member) for member in first)),
        ("row", "col"),
        split_axis=0,
        concat_axis=1,
        tiled=True,
    )
    third = lax.all_to_all(
        tuple((mirror_tail(member, col_devices, row_devices) for member in second)),
        "col",
        split_axis=1,
        concat_axis=0,
        tiled=True,
    )
    return tuple(
        (
            mirror_finish(member, count_planes, row_devices)
            for member, count_planes in zip(third, planes)
        )
    )


def on_device(features, conv_first, conv_second, head_weight, head_bias, cotangent):
    channels, col_count, row_count = features.shape
    length = col_count * lax.axis_size("col")
    cell_count = float(length * length)
    cot_mirror = mirror_half((cotangent,))[0]
    wide_in = widen(features)
    act_first = convolve(wide_in, conv_first, col_count, row_count, False)
    normed_first, inverse_first = normalize(act_first, cell_count)
    hidden_first = elu_apply(normed_first).astype(jnp.bfloat16)
    wide_hidden = widen(hidden_first)
    act_second = convolve(wide_hidden, conv_second, col_count, row_count, False)
    normed_second, inverse_second = normalize(act_second, cell_count)
    summed = normed_second + features.astype(jnp.float32)
    hidden = elu_apply(summed).astype(jnp.bfloat16)
    flat_hidden = hidden.reshape(channels, -1)
    raw_logits = (
        jnp.dot(head_weight, flat_hidden, preferred_element_type=jnp.float32) + head_bias[:, None]
    ).reshape(-1, col_count, row_count)
    logit_mirror = mirror_full((raw_logits,))[0]
    logits = (0.5 * (raw_logits + logit_mirror)).astype(jnp.bfloat16)
    grad_sym = (0.5 * (cotangent.astype(jnp.float32) + cot_mirror.astype(jnp.float32))).astype(
        jnp.bfloat16
    )
    flat_sym = grad_sym.reshape(grad_sym.shape[0], -1)
    bias_term = jnp.sum(flat_sym, axis=1, dtype=jnp.float32)
    head_term = lax.dot_general(
        flat_sym, flat_hidden, (((1,), (1,)), ((), ())), preferred_element_type=jnp.float32
    )
    grad_hidden = jnp.dot(head_weight.T, flat_sym, preferred_element_type=jnp.float32).reshape(
        channels, col_count, row_count
    )
    grad_summed = grad_hidden * elu_slope(summed)
    grad_act_second = norm_back(grad_summed, normed_second, inverse_second, cell_count).astype(
        jnp.bfloat16
    )
    second_term = weight_terms(grad_act_second, wide_hidden, col_count, row_count)
    grad_hidden_first = convolve(
        widen_grad(grad_act_second), conv_second, col_count, row_count, True
    )
    grad_normed_first = grad_hidden_first * elu_slope(normed_first)
    grad_act_first = norm_back(grad_normed_first, normed_first, inverse_first, cell_count).astype(
        jnp.bfloat16
    )
    first_term = weight_terms(grad_act_first, wide_in, col_count, row_count)
    input_grad = (
        convolve(widen_grad(grad_act_first), conv_first, col_count, row_count, True) + grad_summed
    ).astype(jnp.bfloat16)
    reduced = lax.psum((first_term, second_term, head_term, bias_term), ("row", "col"))
    inverse_len = 1.0 / length
    return (
        logits,
        input_grad,
        reduced[0] * inverse_len,
        reduced[1] * inverse_len,
        reduced[2] * inverse_len,
        reduced[3] * inverse_len,
    )


def solution(mesh):
    placed = (P(None, "col", "row"), P(), P(), P(), P(), P(None, "col", "row"))
    return jax.shard_map(
        on_device,
        mesh=mesh,
        in_specs=placed,
        out_specs=(P(None, "col", "row"), P(None, "col", "row"), P(), P(), P(), P()),
        check_vma=False,
    )
```

profile of v0, /device:TPU:1, one launch (start us, length us, event | category | flops | bytes accessed | tf_op | source)
XLA Modules:
  0.0 945.5 jit_solution(8504347659862040630)
XLA Ops:
  12.6 5.3 collective-permute-start
  21.0 7.8 all-to-all-start.3
  35.7 3.5 collective-permute-start.2
  45.4 7.2 collective-permute-done.3
  52.6 3.2 maximum_maximum_fusion
  63.5 67.2 %psum.84 = f32[64]{0:T(128)S(1)} all-reduce(f32[64]{0:T(128)S(1)} %get-tuple-element.108), channel_id=1, replica_groups=mesh['row'=8,'col'=16] {'row','col'}, use_global_device_ids=true, to_apply=%region_1.0 | all-reduce | flops 64 | bytes 512 | tf_op jit(solution)/shard_map/psum | solution.py:84
  131.1 63.5 %psum.85 = f32[64]{0:T(128)S(1)} all-reduce(f32[64]{0:T(128)S(1)} %multiply_reduce_fusion.2), channel_id=1, replica_groups=mesh['row'=8,'col'=16] {'row','col'}, use_global_device_ids=true, to_apply=%region_3.0 | all-reduce | flops 64 | bytes 512 | tf_op jit(solution)/shard_map/psum | solution.py:87
  206.5 3.4 copy.243
  209.8 4.3 collective-permute-done.5
  214.1 3.4 copy.244
  220.2 3.9 collective-permute-start.7
  229.6 3.4 reshape.289
  233.1 11.2 %all-to-all-start.4 = ((bf16[128,2,1184]{2,1,0:T(2,128)(2,1)}), bf16[128,2,1184]{2,1,0:T(2,128)(2,1)}, u32[]{:S(2)}, u32[]{:S(2)}) async-start(bf16[128,2,1184]{2,1,0:T(2,128)(2,1)} %reshape.289), calls=%async_computation.4 | async-start | bytes 1310720 | tf_op jit(solution)/shard_map/all_to_all | solution.py:136
  247.3 4.2 pad_maximum_fusion.1
  260.6 67.2 %psum.86 = f32[64]{0:T(128)S(1)} all-reduce(f32[64]{0:T(128)S(1)} %get-tuple-element.110), channel_id=1, replica_groups=mesh['row'=8,'col'=16] {'row','col'}, use_global_device_ids=true, to_apply=%region_5.6 | all-reduce | flops 64 | bytes 512 | tf_op jit(solution)/shard_map/psum | solution.py:84
  327.7 6.2 reshape.290
  336.5 4.3 all-to-all-start.5
  342.8 65.3 %psum.87 = f32[64]{0:T(128)S(1)} all-reduce(f32[64]{0:T(128)S(1)} %fusion.19), channel_id=1, replica_groups=mesh['row'=8,'col'=16] {'row','col'}, use_global_device_ids=true, to_apply=%region_7.8 | all-reduce | flops 64 | bytes 512 | tf_op jit(solution)/shard_map/psum | solution.py:87
  409.4 12.2 %reshape.288 = f32[128,8,37,8]{3,2,1,0:T(8,128)} reshape(f32[16,8,1,8,296]{4,3,1,0,2:T(8,128)} %convert_bitcast_fusion) | data formatting | bytes 2424832 | tf_op jit(solution)/shard_map/convert_element_type | solution.py:211
  421.5 11.1 %copy.273 = f32[37,8,8,128]{3,2,1,0:T(8,128)S(1)} copy(f32[37,8,8,128]{2,0,1,3:T(8,128)} %bitcast.528) | data formatting | bytes 2424832 | tf_op jit(solution)/shard_map/convert_element_type | solution.py:211
  436.2 3.2 fusion.228
  439.4 62.9 %all-reduce.1 = (f32[64]{0:T(128)S(1)}, f32[64]{0:T(128)S(1)}) all-reduce(f32[64]{0:T(128)S(1)} %get-tuple-element.39, f32[64]{0:T(128)S(1)} %get-tuple-element.38), channel_id=1, replica_groups=mesh['row'=8,'col'=16] {'row','col'}, use_global_device_ids=true, to_apply=%region_11.12 | all-reduce | flops 128 | bytes 1024 | tf_op jit(solution)/shard_map/psum | solution.py:93
  524.1 4.7 collective-permute-start.8
  530.4 3.2 fusion.25
  534.9 3.7 copy.258
  538.7 5.1 copy.259
  546.9 5.3 all-to-all-start
  552.5 3.4 copy.277
  555.9 3.4 copy.278
  561.2 3.5 collective-permute-start.11
  568.5 8.1 collective-permute-done.11
  576.5 7.2 collective-permute-done.10
  583.7 3.2 maximum_maximum_fusion.2
  595.0 67.2 %all-reduce = (f32[64]{0:T(128)S(1)}, f32[64]{0:T(128)S(1)}, f32[37,64]{1,0:T(8,128)S(1)}, f32[37]{0:T(128)S(1)}) all-reduce(f32[64]{0:T(128)S(1)} %get-tuple-element.37, f32[64]{0:T(128)S(1)} %get-tuple-element.36, f32[37,64]{1,0:T(8,128)S(1)} %convolution_bitcast_fusion.23, ...), channel_id=1, replica_groups=mesh['row'=8,'col'=16] {'row','col'}, use_global_device_ids=true, to_apply=%region_15.16 | all-reduce | flops 2533 | bytes 20264 | tf_op jit(solution)/shard_map/psum | solution.py:93
  680.8 5.1 collective-permute-start.12
  686.4 3.2 collective-permute-done.12
  689.6 3.4 copy.293
  692.9 3.4 copy.294
  699.2 4.6 collective-permute-start.15
  708.2 125.5 %all-reduce.5.cloned.1.call-done = (f32[9,64,64]{2,1,0:T(8,128)}, f32[9,64,64]{2,1,0:T(8,128)}) async-done(((f32[9,64,64]{2,1,0:T(8,128)}, f32[9,64,64]{2,1,0:T(8,128)}), (f32[9,64,64]{2,1,0:T(8,128)}, f32[9,64,64]{2,1,0:T(8,128)})) %all-reduce.5.cloned.1.call-update) | async-done | bytes 294928 | tf_op jit(solution)/shard_map/psum | solution.py:238
  837.1 4.8 maximum_maximum_fusion.3
  848.5 4.2 copy.261
  852.7 7.4 all-to-all-start.1
  866.1 17.9 %all-to-all-done.1 = f32[1024,1,296]{2,1,0:T(1,128)} async-done(((f32[1024,1,296]{2,1,0:T(1,128)}), f32[1024,1,296]{2,1,0:T(1,128)}, u32[]{:S(2)}, u32[]{:S(2)}) %all-to-all-start.1) | async-done | bytes 1212448 | tf_op jit(solution)/shard_map/all_to_all | solution.py:169
  887.0 5.5 all-to-all-start.2
  898.6 15.5 %all-to-all-done.2 = f32[8,16,8,296]{3,2,0,1:T(8,128)} async-done(((f32[8,16,8,296]{3,2,0,1:T(8,128)}), f32[8,16,8,296]{3,2,0,1:T(8,128)}, u32[]{:S(2)}, u32[]{:S(2)}) %all-to-all-start.2) | async-done | bytes 1212448 | tf_op jit(solution)/shard_map/all_to_all | solution.py:176
  914.1 12.2 %reshape.287 = f32[128,8,37,8]{3,2,1,0:T(8,128)} reshape(f32[16,8,1,8,296]{4,3,1,0,2:T(8,128)} %bitcast.32) | data formatting | bytes 2424832 | tf_op jit(solution)/shard_map/reshape | solution.py:121
  926.2 11.2 %copy.265 = f32[37,8,8,128]{3,2,1,0:T(8,128)S(1)} copy(f32[37,8,8,128]{2,0,1,3:T(8,128)} %bitcast.529) | data formatting | bytes 2424832 | tf_op jit(solution)/shard_map/transpose | solution.py:121
  (245 shorter events, 164.8 us)
Async XLA Ops:
  7.2 427.7 %copy-start = (bf16[37,64]{1,0:T(8,128)(2,1)S(1)}, bf16[37,64]{1,0:T(8,128)(2,1)}, u32[]{:S(2)}) copy-start(bf16[37,64]{1,0:T(8,128)(2,1)} %param.9) | copy-start | bytes 14212
  9.2 8.7 copy-start.43
  10.3 22.0 %collective-permute-start.1 = (bf16[64,64,16]{1,2,0:T(8,128)(2,1)}, bf16[64,64,16]{1,2,0:T(8,128)(2,1)}, u32[]{:S(2)}, u32[]{:S(2)}) collective-permute-start(bf16[64,64,16]{1,2,0:T(8,128)(2,1)} %copy.320), channel_id=1, source_target_pairs={{16,0},{32,16},{48,32},{64,48},{80,64},{96,80},{112,96},{17,1},{33... | collective-permute-start | bytes 393224 | tf_op jit(solution)/shard_map/ppermute | solution.py:18
  12.6 16.9 %collective-permute-start = (bf16[64,64,16]{1,2,0:T(8,128)(2,1)}, bf16[64,64,16]{1,2,0:T(8,128)(2,1)}, u32[]{:S(2)}, u32[]{:S(2)}) collective-permute-start(bf16[64,64,16]{1,2,0:T(8,128)(2,1)} %copy.319), channel_id=1, source_target_pairs={{0,16},{16,32},{32,48},{48,64},{64,80},{80,96},{96,112},{1,17},{17... | collective-permute-start | bytes 393224 | tf_op jit(solution)/shard_map/ppermute | solution.py:15
  19.6 9.2 copy-start.15
  21.0 205.0 %all-to-all-start.3 = ((bf16[16,64,296]{2,1,0:T(8,128)(2,1)}), bf16[16,64,296]{2,1,0:T(8,128)(2,1)}, u32[]{:S(2)}, u32[]{:S(2)}) async-start(bf16[16,64,296]{2,1,0:T(8,128)(2,1)} %copy.268), calls=%async_computation.3 | async-start | bytes 1572864 | tf_op jit(solution)/shard_map/all_to_all | solution.py:129
  29.6 23.1 %copy-start.4 = (bf16[64,64,128]{2,0,1:T(8,128)(2,1)}, bf16[64,64,128]{2,0,1:T(8,128)(2,1)S(1)}, u32[]{:S(2)}) copy-start(bf16[64,64,128]{2,0,1:T(8,128)(2,1)S(1)} %copy.226) | copy-start | bytes 3145732
  32.3 20.3 %copy-start.9 = (bf16[64,64,16]{2,0,1:T(8,128)(2,1)}, bf16[64,64,16]{2,0,1:T(8,128)(2,1)S(1)}, u32[]{:S(2)}) copy-start(bf16[64,64,16]{2,0,1:T(8,128)(2,1)S(1)} %copy.225) | copy-start | bytes 393220
  35.1 17.6 %copy-start.7 = (bf16[64,64,16]{2,0,1:T(8,128)(2,1)}, bf16[64,64,16]{2,0,1:T(8,128)(2,1)S(1)}, u32[]{:S(2)}) copy-start(bf16[64,64,16]{2,0,1:T(8,128)(2,1)S(1)} %copy.227) | copy-start | bytes 393220
  35.7 9.7 %collective-permute-start.2 = (bf16[64,16,160]{2,0,1:T(8,128)(2,1)S(1)}, bf16[64,16,160]{2,0,1:T(8,128)(2,1)S(1)}, u32[]{:S(2)}, u32[]{:S(2)}) collective-permute-start(bf16[64,16,160]{2,0,1:T(8,128)(2,1)S(1)} %get-tuple-element.66), channel_id=1, source_target_pairs={{0,1},{1,2},{2,3},{3,4},{4,5},{5,6},{6,7},{7,8},{8,9},{9,10},{10,1... | collective-permute-start | bytes 983048 | tf_op jit(solution)/shard_map/ppermute | solution.py:15
  39.3 3.5 copy-start.45
  39.3 13.3 %collective-permute-start.3 = (bf16[64,16,160]{2,0,1:T(8,128)(2,1)S(1)}, bf16[64,16,160]{2,0,1:T(8,128)(2,1)S(1)}, u32[]{:S(2)}, u32[]{:S(2)}) collective-permute-start(bf16[64,16,160]{2,0,1:T(8,128)(2,1)S(1)} %get-tuple-element.67), channel_id=1, source_target_pairs={{1,0},{2,1},{3,2},{4,3},{5,4},{6,5},{7,6},{8,7},{9,8},{10,9},{11,1... | collective-permute-start | bytes 983048 | tf_op jit(solution)/shard_map/ppermute | solution.py:18
  195.2 52.0 %copy-start.2 = (bf16[64,64,128]{2,0,1:T(8,128)(2,1)}, bf16[64,64,128]{2,0,1:T(8,128)(2,1)S(1)}, u32[]{:S(2)}) copy-start(bf16[64,64,128]{2,0,1:T(8,128)(2,1)S(1)} %fusion.5) | copy-start | bytes 3145732
  199.3 7.2 collective-permute-start.4
  205.2 8.9 collective-permute-start.5
  220.2 27.0 %collective-permute-start.7 = (bf16[64,16,160]{2,0,1:T(8,128)(2,1)}, bf16[64,16,160]{2,0,1:T(8,128)(2,1)}, u32[]{:S(2)}, u32[]{:S(2)}) collective-permute-start(bf16[64,16,160]{2,0,1:T(8,128)(2,1)} %get-tuple-element.62), channel_id=1, source_target_pairs={{1,0},{2,1},{3,2},{4,3},{5,4},{6,5},{7,6},{8,7},{9,8},{10,9},{11,1... | collective-permute-start | bytes 983048 | tf_op jit(solution)/shard_map/ppermute | solution.py:18
  224.1 23.1 %collective-permute-start.6 = (bf16[64,16,160]{2,0,1:T(8,128)(2,1)}, bf16[64,16,160]{2,0,1:T(8,128)(2,1)}, u32[]{:S(2)}, u32[]{:S(2)}) collective-permute-start(bf16[64,16,160]{2,0,1:T(8,128)(2,1)} %get-tuple-element.63), channel_id=1, source_target_pairs={{0,1},{1,2},{2,3},{3,4},{4,5},{5,6},{6,7},{7,8},{8,9},{9,10},{10,1... | collective-permute-start | bytes 983048 | tf_op jit(solution)/shard_map/ppermute | solution.py:15
  233.1 94.7 %all-to-all-start.4 = ((bf16[128,2,1184]{2,1,0:T(2,128)(2,1)}), bf16[128,2,1184]{2,1,0:T(2,128)(2,1)}, u32[]{:S(2)}, u32[]{:S(2)}) async-start(bf16[128,2,1184]{2,1,0:T(2,128)(2,1)} %reshape.289), calls=%async_computation.4 | async-start | bytes 1310720 | tf_op jit(solution)/shard_map/all_to_all | solution.py:136
  244.3 3.0 copy-start.11
  244.3 3.0 copy-start.13
  336.5 71.6 %all-to-all-start.5 = ((bf16[8,16,8,296]{3,2,0,1:T(8,128)(2,1)}), bf16[8,16,8,296]{3,2,0,1:T(8,128)(2,1)S(1)}, u32[]{:S(2)}, u32[]{:S(2)}) async-start(bf16[8,16,8,296]{3,2,0,1:T(8,128)(2,1)} %copy.271), calls=%async_computation.5 | async-start | bytes 1572864 | tf_op jit(solution)/shard_map/all_to_all | solution.py:143
  502.3 3.0 copy-start.28
  517.0 11.8 %copy-start.48 = (f32[37]{0:T(128)S(1)}, f32[37]{0:T(128)}, u32[]{:S(2)}) copy-start(f32[37]{0:T(128)} %param.10) | copy-start | bytes 448
  522.8 33.1 %collective-permute-start.9 = (bf16[64,64,16]{1,2,0:T(8,128)(2,1)}, bf16[64,64,16]{1,2,0:T(8,128)(2,1)}, u32[]{:S(2)}, u32[]{:S(2)}) collective-permute-start(bf16[64,64,16]{1,2,0:T(8,128)(2,1)} %copy.276), channel_id=1, source_target_pairs={{16,0},{32,16},{48,32},{64,48},{80,64},{96,80},{112,96},{17,1},{33... | collective-permute-start | bytes 393224 | tf_op jit(solution)/shard_map/ppermute | solution.py:18
  524.1 28.4 %collective-permute-start.8 = (bf16[64,64,16]{1,2,0:T(8,128)(2,1)}, bf16[64,64,16]{1,2,0:T(8,128)(2,1)}, u32[]{:S(2)}, u32[]{:S(2)}) collective-permute-start(bf16[64,64,16]{1,2,0:T(8,128)(2,1)} %copy.275), channel_id=1, source_target_pairs={{0,16},{16,32},{32,48},{48,64},{64,80},{80,96},{96,112},{1,17},{17... | collective-permute-start | bytes 393224 | tf_op jit(solution)/shard_map/ppermute | solution.py:15
  530.4 4.6 copy-start.33
  546.9 301.6 %all-to-all-start = ((f32[16,64,296]{2,1,0:T(8,128)}), f32[16,64,296]{2,1,0:T(8,128)}, u32[]{:S(2)}, u32[]{:S(2)}) async-start(f32[16,64,296]{2,1,0:T(8,128)} %copy.260), calls=%async_computation | async-start | bytes 3145728 | tf_op jit(solution)/shard_map/all_to_all | solution.py:162
  552.3 281.4 %all-reduce.5.cloned.1.call-start = ((), (), s32[]{:S(2)}) async-start(), calls=%async_computation.6 | async-start | bytes 1179648 | tf_op jit(solution)/shard_map/psum | solution.py:238
  559.3 7.5 copy-start.34
  559.3 7.5 copy-start.36
  559.3 8.0 copy-start.23
  559.3 8.0 copy-start.24
  561.2 15.3 %collective-permute-start.11 = (bf16[64,16,160]{2,0,1:T(8,128)(2,1)S(1)}, bf16[64,16,160]{2,0,1:T(8,128)(2,1)S(1)}, u32[]{:S(2)}, u32[]{:S(2)}) collective-permute-start(bf16[64,16,160]{2,0,1:T(8,128)(2,1)S(1)} %get-tuple-element.58), channel_id=1, source_target_pairs={{0,1},{1,2},{2,3},{3,4},{4,5},{5,6},{6,7},{7,8},{8,9},{9,10},{10,1... | collective-permute-start | bytes 983048 | tf_op jit(solution)/shard_map/ppermute | solution.py:15
  564.8 18.9 %collective-permute-start.10 = (bf16[64,16,160]{2,0,1:T(8,128)(2,1)S(1)}, bf16[64,16,160]{2,0,1:T(8,128)(2,1)S(1)}, u32[]{:S(2)}, u32[]{:S(2)}) collective-permute-start(bf16[64,16,160]{2,0,1:T(8,128)(2,1)S(1)} %get-tuple-element.59), channel_id=1, source_target_pairs={{1,0},{2,1},{3,2},{4,3},{5,4},{6,5},{7,6},{8,7},{9,8},{10,9},{11,1... | collective-permute-start | bytes 983048 | tf_op jit(solution)/shard_map/ppermute | solution.py:18
  662.2 2.7 copy-start.32
  673.5 12.3 %copy-start.47 = (f32[9,64,64]{2,1,0:T(8,128)}, f32[9,64,64]{2,1,0:T(8,128)S(1)}, u32[]{:S(2)}) copy-start(f32[9,64,64]{2,1,0:T(8,128)S(1)} %fusion.34) | copy-start | bytes 442372
  679.5 13.4 %collective-permute-start.13 = (bf16[64,64,16]{1,2,0:T(8,128)(2,1)}, bf16[64,64,16]{1,2,0:T(8,128)(2,1)}, u32[]{:S(2)}, u32[]{:S(2)}) collective-permute-start(bf16[64,64,16]{1,2,0:T(8,128)(2,1)} %copy.292), channel_id=1, source_target_pairs={{16,0},{32,16},{48,32},{64,48},{80,64},{96,80},{112,96},{17,1},{33... | collective-permute-start | bytes 393224 | tf_op jit(solution)/shard_map/ppermute | solution.py:18
  680.8 8.8 collective-permute-start.12
  696.3 9.4 copy-start.21
  696.3 9.4 copy-start.22
  699.2 137.9 %collective-permute-start.15 = (bf16[64,16,160]{2,0,1:T(8,128)(2,1)}, bf16[64,16,160]{2,0,1:T(8,128)(2,1)}, u32[]{:S(2)}, u32[]{:S(2)}) collective-permute-start(bf16[64,16,160]{2,0,1:T(8,128)(2,1)} %get-tuple-element.54), channel_id=1, source_target_pairs={{0,1},{1,2},{2,3},{3,4},{4,5},{5,6},{6,7},{7,8},{8,9},{9,10},{10,1... | collective-permute-start | bytes 983048 | tf_op jit(solution)/shard_map/ppermute | solution.py:15
  703.8 133.3 %collective-permute-start.14 = (bf16[64,16,160]{2,0,1:T(8,128)(2,1)}, bf16[64,16,160]{2,0,1:T(8,128)(2,1)}, u32[]{:S(2)}, u32[]{:S(2)}) collective-permute-start(bf16[64,16,160]{2,0,1:T(8,128)(2,1)} %get-tuple-element.55), channel_id=1, source_target_pairs={{1,0},{2,1},{3,2},{4,3},{5,4},{6,5},{7,6},{8,7},{9,8},{10,9},{11,1... | collective-permute-start | bytes 983048 | tf_op jit(solution)/shard_map/ppermute | solution.py:18
  844.2 2.5 copy-start.39
  852.7 31.3 %all-to-all-start.1 = ((f32[1024,1,296]{2,1,0:T(1,128)}), f32[1024,1,296]{2,1,0:T(1,128)}, u32[]{:S(2)}, u32[]{:S(2)}) async-start(f32[1024,1,296]{2,1,0:T(1,128)} %copy.261), calls=%async_computation.1 | async-start | bytes 3145728 | tf_op jit(solution)/shard_map/all_to_all | solution.py:169
  860.1 2.5 copy-start.42
  887.0 27.1 %all-to-all-start.2 = ((f32[8,16,8,296]{3,2,0,1:T(8,128)}), f32[8,16,8,296]{3,2,0,1:T(8,128)}, u32[]{:S(2)}, u32[]{:S(2)}) async-start(f32[8,16,8,296]{3,2,0,1:T(8,128)} %copy.263), calls=%async_computation.2 | async-start | bytes 3145728 | tf_op jit(solution)/shard_map/all_to_all | solution.py:176
  926.2 11.2 %copy-start.37 = (f32[5,8,64,128]{3,2,1,0:T(8,128)S(1)}, f32[5,8,64,128]{3,2,1,0:T(8,128)}, u32[]{:S(2)}) copy-start(f32[5,8,64,128]{3,2,1,0:T(8,128)} %copy.361) | copy-start | bytes 3932164
  926.2 12.2 %copy-start.1 = (bf16[37,64]{1,0:T(8,128)(2,1)S(1)}, bf16[37,64]{1,0:T(8,128)(2,1)}, u32[]{:S(2)}) copy-start(bf16[37,64]{1,0:T(8,128)(2,1)} %param.9) | copy-start | bytes 14212
  (24 other events, 40.2 us)
Sparse Core Ops, SparseCore 0:
  686.0 147.6 all-reduce.4
where the time goes:
time: 954 us; the launch traced here: 946 us
  blocking collectives  393 us (41%)
  waiting for transfers between devices  191 us (20%)
  local copies, waits for them, and re-layouts  156 us (16%)
  starting transfers between devices  88.6 us (9%)
  other arithmetic  55 us (6%)
  matrix products  46.3 us (5%)
  between operations  15.3 us (2%)
    psum x2, blocking collectives, normalize(): totals = lax.psum(jnp.sum(activation, axis=(1, 2)), ('row', 'col'))  134 us
    psum x2, blocking collectives, norm_back(): lax.psum((jnp.sum(gradient, axis=(1, 2)), jnp.sum(gradient * normed, axis...  130 us
    psum x2, blocking collectives, normalize(): lax.psum(jnp.sum(centered * centered, axis=(1, 2)), ('row', 'col'))  129 us
    psum x1, waiting for transfers between devices, on_device(): lax.psum((first_term, second_term, head_term, bias_term), ('row', 'col'))  125 us
    unnamed x117, local copies, waits for them, and re-layouts  38.8 us
    ppermute x8, starting transfers between devices, with_halo(): lax.ppermute(lax.slice_in_dim(block, block.shape[dim] - width, None, axis...  31.6 us
    dot_general x36, matrix products, convolve(): jnp.dot(matrix, window, preferred_element_type=jnp.float32)  25.6 us
    convert_element_type x2, local copies, waits for them, and re-layouts, on_device(): cot_mirror.astype(jnp.float32)  23.2 us
  transfers between devices with their start and end apart: 23, of which 9 were waited for; matrix products, arithmetic and copies ran while one was open for 16% of the time, Pallas kernels for 0%

commit v1 on v0

--- a/solution.py
+++ b/solution.py
@@ -90,8 +90,14 @@
 
 
 def norm_back(gradient, normed, inverse_std, cell_count):
-    first_sum, second_sum = lax.psum(
-        (jnp.sum(gradient, axis=(1, 2)), jnp.sum(gradient * normed, axis=(1, 2))), ("row", "col")
+
+    def _pack_pairs_all(x_in):
+        for ix in ("col", "row"):
+            x_in = lax.psum(x_in, ix)
+        return x_in
+
+    first_sum, second_sum = _pack_pairs_all(
+        (jnp.sum(gradient, axis=(1, 2)), jnp.sum(gradient * normed, axis=(1, 2)))
     )
     first_mean = first_sum / cell_count
     second_mean = second_sum / cell_count

time: 954 us -> 983 us (1.030)
  blocking collectives: 393 us -> 425 us
  starting transfers between devices: 88.6 us -> 99.9 us
    psum x2 -> x5, blocking collectives: 130 us -> 162 us  [the longest x4 85.5 us: _pack_pairs_all(): x_in = lax.psum(x_in, ix)]
    unnamed x117 -> x119, local copies, waits for them, and re-layouts: 38.8 us -> 41.5 us
  transfers between devices with their start and end apart: 23 -> 23, of which waited for: 9 -> 8; matrix products, arithmetic and copies ran while one was open for 16% -> 15% of each run, Pallas kernels for 0% -> 0%
where the time goes in v1:
time: 983 us; the launch traced here: 974 us
  blocking collectives  425 us (43%)
  waiting for transfers between devices  182 us (19%)
  local copies, waits for them, and re-layouts  159 us (16%)
  starting transfers between devices  99.9 us (10%)
  other arithmetic  55.2 us (6%)
  matrix products  39 us (4%)
  between operations  15.4 us (2%)
    psum x2, blocking collectives, normalize(): totals = lax.psum(jnp.sum(activation, axis=(1, 2)), ('row', 'col'))  134 us
    psum x2, blocking collectives, normalize(): lax.psum(jnp.sum(centered * centered, axis=(1, 2)), ('row', 'col'))  129 us
    psum x1, waiting for transfers between devices, on_device(): lax.psum((first_term, second_term, head_term, bias_term), ('row', 'col'))  125 us
    psum x4, blocking collectives, _pack_pairs_all(): x_in = lax.psum(x_in, ix)  85.5 us
    psum x1, blocking collectives, on_device(): lax.psum((first_term, second_term, head_term, bias_term), ('row', 'col'))  76 us
    unnamed x119, local copies, waits for them, and re-layouts  41.5 us
    ppermute x8, starting transfers between devices, with_halo(): lax.ppermute(lax.slice_in_dim(block, block.shape[dim] - width, None, axis...  34.7 us
    dot_general x36, matrix products, convolve(): jnp.dot(matrix, window, preferred_element_type=jnp.float32)  25.6 us
  transfers between devices with their start and end apart: 23, of which 8 were waited for; matrix products, arithmetic and copies ran while one was open for 15% of the time, Pallas kernels for 0%

profile of v1, /device:TPU:1, one launch (start us, length us, event | category | flops | bytes accessed | tf_op | source)
XLA Modules:
  0.0 974.4 jit_solution(11505383016378026617)
XLA Ops:
  12.6 5.3 collective-permute-start
  21.1 7.8 all-to-all-start.3
  35.8 3.5 collective-permute-start.2
  45.4 7.2 collective-permute-done.3
  52.7 3.2 maximum_maximum_fusion
  63.5 67.2 %psum.112 = f32[64]{0:T(128)S(1)} all-reduce(f32[64]{0:T(128)S(1)} %get-tuple-element.112), channel_id=1, replica_groups=mesh['row'=8,'col'=16] {'row','col'}, use_global_device_ids=true, to_apply=%region_1.0 | all-reduce | flops 64 | bytes 512 | tf_op jit(solution)/shard_map/psum | solution.py:84
  131.1 63.4 %psum.113 = f32[64]{0:T(128)S(1)} all-reduce(f32[64]{0:T(128)S(1)} %multiply_reduce_fusion.2), channel_id=1, replica_groups=mesh['row'=8,'col'=16] {'row','col'}, use_global_device_ids=true, to_apply=%region_3.0 | all-reduce | flops 64 | bytes 512 | tf_op jit(solution)/shard_map/psum | solution.py:87
  206.5 3.4 copy.243
  209.9 4.2 collective-permute-done.5
  214.1 3.4 copy.244
  220.2 4.0 collective-permute-start.7
  229.7 3.4 reshape.289
  233.1 11.2 %all-to-all-start.4 = ((bf16[128,2,1184]{2,1,0:T(2,128)(2,1)}), bf16[128,2,1184]{2,1,0:T(2,128)(2,1)}, u32[]{:S(2)}, u32[]{:S(2)}) async-start(bf16[128,2,1184]{2,1,0:T(2,128)(2,1)} %reshape.289), calls=%async_computation.4 | async-start | bytes 1310720 | tf_op jit(solution)/shard_map/all_to_all | solution.py:142
  247.3 4.2 pad_maximum_fusion.1
  260.7 67.2 %psum.114 = f32[64]{0:T(128)S(1)} all-reduce(f32[64]{0:T(128)S(1)} %get-tuple-element.114), channel_id=1, replica_groups=mesh['row'=8,'col'=16] {'row','col'}, use_global_device_ids=true, to_apply=%region_5.6 | all-reduce | flops 64 | bytes 512 | tf_op jit(solution)/shard_map/psum | solution.py:84
  327.9 6.2 reshape.290
  336.6 4.3 all-to-all-start.5
  342.9 65.3 %psum.115 = f32[64]{0:T(128)S(1)} all-reduce(f32[64]{0:T(128)S(1)} %fusion.19), channel_id=1, replica_groups=mesh['row'=8,'col'=16] {'row','col'}, use_global_device_ids=true, to_apply=%region_7.8 | all-reduce | flops 64 | bytes 512 | tf_op jit(solution)/shard_map/psum | solution.py:87
  409.5 12.2 %reshape.288 = f32[128,8,37,8]{3,2,1,0:T(8,128)} reshape(f32[16,8,1,8,296]{4,3,1,0,2:T(8,128)} %convert_bitcast_fusion) | data formatting | bytes 2424832 | tf_op jit(solution)/shard_map/convert_element_type | solution.py:217
  421.7 11.1 %copy.273 = f32[37,8,8,128]{3,2,1,0:T(8,128)S(1)} copy(f32[37,8,8,128]{2,0,1,3:T(8,128)} %bitcast.528) | data formatting | bytes 2424832 | tf_op jit(solution)/shard_map/convert_element_type | solution.py:217
  436.3 3.2 fusion.228
  439.5 27.4 %all-reduce.3 = (f32[64]{0:T(128)S(1)}, f32[64]{0:T(128)S(1)}) all-reduce(f32[64]{0:T(128)S(1)} %get-tuple-element.39, f32[64]{0:T(128)S(1)} %get-tuple-element.38), channel_id=1, replica_groups=mesh['row'=8,'col'=16] {'col'}, use_global_device_ids=true, to_apply=%region_12.13 | all-reduce | flops 128 | bytes 1024 | tf_op jit(solution)/shard_map/psum | solution.py:96
  466.9 17.8 %all-reduce.5 = (f32[64]{0:T(128)S(1)}, f32[64]{0:T(128)S(1)}) all-reduce(f32[64]{0:T(128)S(1)} %get-tuple-element.46, f32[64]{0:T(128)S(1)} %get-tuple-element.47), channel_id=1, replica_groups=mesh['row'=8,'col'=16] {'row'}, use_global_device_ids=true, to_apply=%region_13.14 | all-reduce | flops 128 | bytes 1024 | tf_op jit(solution)/shard_map/psum | solution.py:96
  505.8 4.7 collective-permute-start.8
  510.5 3.7 copy.258
  514.3 5.2 copy.259
  522.5 9.9 %all-to-all-start = ((f32[16,64,296]{2,1,0:T(8,128)}), f32[16,64,296]{2,1,0:T(8,128)}, u32[]{:S(2)}, u32[]{:S(2)}) async-start(f32[16,64,296]{2,1,0:T(8,128)} %copy.260), calls=%async_computation | async-start | bytes 3145728 | tf_op jit(solution)/shard_map/all_to_all | solution.py:168
  532.5 76.0 %all-reduce = (f32[37,64]{1,0:T(8,128)S(1)}, f32[37]{0:T(128)S(1)}) all-reduce(f32[37,64]{1,0:T(8,128)S(1)} %convolution_bitcast_fusion.23, f32[37]{0:T(128)S(1)} %get-tuple-element.52), channel_id=1, replica_groups=mesh['row'=8,'col'=16] {'row','col'}, use_global_device_ids=true, to_apply=%region_22.23 | all-reduce | flops 2405 | bytes 19240 | tf_op jit(solution)/shard_map/psum | solution.py:244
  609.1 3.4 copy.277
  612.5 3.4 copy.278
  626.9 7.2 collective-permute-done.10
  634.2 3.2 maximum_maximum_fusion.2
  645.4 22.6 %all-reduce.2 = (f32[64]{0:T(128)S(1)}, f32[64]{0:T(128)S(1)}) all-reduce(f32[64]{0:T(128)S(1)} %get-tuple-element.37, f32[64]{0:T(128)S(1)} %get-tuple-element.36), channel_id=1, replica_groups=mesh['row'=8,'col'=16] {'col'}, use_global_device_ids=true, to_apply=%region_18.19 | all-reduce | flops 128 | bytes 1024 | tf_op jit(solution)/shard_map/psum | solution.py:96
  668.1 17.7 %all-reduce.4 = (f32[64]{0:T(128)S(1)}, f32[64]{0:T(128)S(1)}) all-reduce(f32[64]{0:T(128)S(1)} %get-tuple-element.44, f32[64]{0:T(128)S(1)} %get-tuple-element.45), channel_id=1, replica_groups=mesh['row'=8,'col'=16] {'row'}, use_global_device_ids=true, to_apply=%region_19.20 | all-reduce | flops 128 | bytes 1024 | tf_op jit(solution)/shard_map/psum | solution.py:96
  703.7 4.7 collective-permute-start.12
  711.3 3.4 copy.293
  714.7 3.4 copy.294
  720.9 8.5 collective-permute-start.15
  729.4 5.8 collective-permute-start.14
  737.8 124.7 %all-reduce.8.cloned.1.call-done = (f32[9,64,64]{2,1,0:T(8,128)}, f32[9,64,64]{2,1,0:T(8,128)}) async-done(((f32[9,64,64]{2,1,0:T(8,128)}, f32[9,64,64]{2,1,0:T(8,128)}), (f32[9,64,64]{2,1,0:T(8,128)}, f32[9,64,64]{2,1,0:T(8,128)})) %all-reduce.8.cloned.1.call-update) | async-done | bytes 294928 | tf_op jit(solution)/shard_map/psum | solution.py:244
  865.9 5.0 maximum_maximum_fusion.3
  877.5 4.2 copy.261
  881.7 7.1 all-to-all-start.1
  894.8 18.1 %all-to-all-done.1 = f32[1024,1,296]{2,1,0:T(1,128)} async-done(((f32[1024,1,296]{2,1,0:T(1,128)}), f32[1024,1,296]{2,1,0:T(1,128)}, u32[]{:S(2)}, u32[]{:S(2)}) %all-to-all-start.1) | async-done | bytes 1212448 | tf_op jit(solution)/shard_map/all_to_all | solution.py:175
  915.8 5.7 all-to-all-start.2
  927.6 15.3 %all-to-all-done.2 = f32[8,16,8,296]{3,2,0,1:T(8,128)} async-done(((f32[8,16,8,296]{3,2,0,1:T(8,128)}), f32[8,16,8,296]{3,2,0,1:T(8,128)}, u32[]{:S(2)}, u32[]{:S(2)}) %all-to-all-start.2) | async-done | bytes 1212448 | tf_op jit(solution)/shard_map/all_to_all | solution.py:182
  942.9 12.2 %reshape.287 = f32[128,8,37,8]{3,2,1,0:T(8,128)} reshape(f32[16,8,1,8,296]{4,3,1,0,2:T(8,128)} %bitcast.32) | data formatting | bytes 2424832 | tf_op jit(solution)/shard_map/reshape | solution.py:127
  955.1 11.2 %copy.265 = f32[37,8,8,128]{3,2,1,0:T(8,128)S(1)} copy(f32[37,8,8,128]{2,0,1,3:T(8,128)} %bitcast.529) | data formatting | bytes 2424832 | tf_op jit(solution)/shard_map/transpose | solution.py:127
  (250 shorter events, 166.9 us)
Async XLA Ops:
  7.2 427.9 %copy-start = (bf16[37,64]{1,0:T(8,128)(2,1)S(1)}, bf16[37,64]{1,0:T(8,128)(2,1)}, u32[]{:S(2)}) copy-start(bf16[37,64]{1,0:T(8,128)(2,1)} %param.9) | copy-start | bytes 14212
  9.2 8.7 copy-start.43
  10.3 22.1 %collective-permute-start.1 = (bf16[64,64,16]{1,2,0:T(8,128)(2,1)}, bf16[64,64,16]{1,2,0:T(8,128)(2,1)}, u32[]{:S(2)}, u32[]{:S(2)}) collective-permute-start(bf16[64,64,16]{1,2,0:T(8,128)(2,1)} %copy.320), channel_id=1, source_target_pairs={{16,0},{32,16},{48,32},{64,48},{80,64},{96,80},{112,96},{17,1},{33... | collective-permute-start | bytes 393224 | tf_op jit(solution)/shard_map/ppermute | solution.py:18
  12.6 16.9 %collective-permute-start = (bf16[64,64,16]{1,2,0:T(8,128)(2,1)}, bf16[64,64,16]{1,2,0:T(8,128)(2,1)}, u32[]{:S(2)}, u32[]{:S(2)}) collective-permute-start(bf16[64,64,16]{1,2,0:T(8,128)(2,1)} %copy.319), channel_id=1, source_target_pairs={{0,16},{16,32},{32,48},{48,64},{64,80},{80,96},{96,112},{1,17},{17... | collective-permute-start | bytes 393224 | tf_op jit(solution)/shard_map/ppermute | solution.py:15
  19.6 9.2 copy-start.15
  21.1 205.0 %all-to-all-start.3 = ((bf16[16,64,296]{2,1,0:T(8,128)(2,1)}), bf16[16,64,296]{2,1,0:T(8,128)(2,1)}, u32[]{:S(2)}, u32[]{:S(2)}) async-start(bf16[16,64,296]{2,1,0:T(8,128)(2,1)} %copy.268), calls=%async_computation.3 | async-start | bytes 1572864 | tf_op jit(solution)/shard_map/all_to_all | solution.py:135
  29.6 23.1 %copy-start.4 = (bf16[64,64,128]{2,0,1:T(8,128)(2,1)}, bf16[64,64,128]{2,0,1:T(8,128)(2,1)S(1)}, u32[]{:S(2)}) copy-start(bf16[64,64,128]{2,0,1:T(8,128)(2,1)S(1)} %copy.226) | copy-start | bytes 3145732
  32.3 20.3 %copy-start.9 = (bf16[64,64,16]{2,0,1:T(8,128)(2,1)}, bf16[64,64,16]{2,0,1:T(8,128)(2,1)S(1)}, u32[]{:S(2)}) copy-start(bf16[64,64,16]{2,0,1:T(8,128)(2,1)S(1)} %copy.225) | copy-start | bytes 393220
  35.1 17.6 %copy-start.7 = (bf16[64,64,16]{2,0,1:T(8,128)(2,1)}, bf16[64,64,16]{2,0,1:T(8,128)(2,1)S(1)}, u32[]{:S(2)}) copy-start(bf16[64,64,16]{2,0,1:T(8,128)(2,1)S(1)} %copy.227) | copy-start | bytes 393220
  35.8 9.7 collective-permute-start.2
  39.3 3.5 copy-start.45
  39.3 13.3 %collective-permute-start.3 = (bf16[64,16,160]{2,0,1:T(8,128)(2,1)S(1)}, bf16[64,16,160]{2,0,1:T(8,128)(2,1)S(1)}, u32[]{:S(2)}, u32[]{:S(2)}) collective-permute-start(bf16[64,16,160]{2,0,1:T(8,128)(2,1)S(1)} %get-tuple-element.71), channel_id=1, source_target_pairs={{1,0},{2,1},{3,2},{4,3},{5,4},{6,5},{7,6},{8,7},{9,8},{10,9},{11,1... | collective-permute-start | bytes 983048 | tf_op jit(solution)/shard_map/ppermute | solution.py:18
  55.9 2.3 copy-start.31
  195.1 52.2 %copy-start.2 = (bf16[64,64,128]{2,0,1:T(8,128)(2,1)}, bf16[64,64,128]{2,0,1:T(8,128)(2,1)S(1)}, u32[]{:S(2)}) copy-start(bf16[64,64,128]{2,0,1:T(8,128)(2,1)S(1)} %fusion.5) | copy-start | bytes 3145732
  199.2 7.3 collective-permute-start.4
  205.2 8.9 collective-permute-start.5
  220.2 27.1 %collective-permute-start.7 = (bf16[64,16,160]{2,0,1:T(8,128)(2,1)}, bf16[64,16,160]{2,0,1:T(8,128)(2,1)}, u32[]{:S(2)}, u32[]{:S(2)}) collective-permute-start(bf16[64,16,160]{2,0,1:T(8,128)(2,1)} %get-tuple-element.66), channel_id=1, source_target_pairs={{1,0},{2,1},{3,2},{4,3},{5,4},{6,5},{7,6},{8,7},{9,8},{10,9},{11,1... | collective-permute-start | bytes 983048 | tf_op jit(solution)/shard_map/ppermute | solution.py:18
  224.2 23.1 %collective-permute-start.6 = (bf16[64,16,160]{2,0,1:T(8,128)(2,1)}, bf16[64,16,160]{2,0,1:T(8,128)(2,1)}, u32[]{:S(2)}, u32[]{:S(2)}) collective-permute-start(bf16[64,16,160]{2,0,1:T(8,128)(2,1)} %get-tuple-element.67), channel_id=1, source_target_pairs={{0,1},{1,2},{2,3},{3,4},{4,5},{5,6},{6,7},{7,8},{8,9},{9,10},{10,1... | collective-permute-start | bytes 983048 | tf_op jit(solution)/shard_map/ppermute | solution.py:15
  233.1 94.7 %all-to-all-start.4 = ((bf16[128,2,1184]{2,1,0:T(2,128)(2,1)}), bf16[128,2,1184]{2,1,0:T(2,128)(2,1)}, u32[]{:S(2)}, u32[]{:S(2)}) async-start(bf16[128,2,1184]{2,1,0:T(2,128)(2,1)} %reshape.289), calls=%async_computation.4 | async-start | bytes 1310720 | tf_op jit(solution)/shard_map/all_to_all | solution.py:142
  244.4 3.0 copy-start.11
  244.4 3.0 copy-start.13
  251.5 2.4 copy-start.27
  336.6 71.6 %all-to-all-start.5 = ((bf16[8,16,8,296]{3,2,0,1:T(8,128)(2,1)}), bf16[8,16,8,296]{3,2,0,1:T(8,128)(2,1)S(1)}, u32[]{:S(2)}, u32[]{:S(2)}) async-start(bf16[8,16,8,296]{3,2,0,1:T(8,128)(2,1)} %copy.271), calls=%async_computation.5 | async-start | bytes 1572864 | tf_op jit(solution)/shard_map/all_to_all | solution.py:149
  484.7 3.0 copy-start.28
  488.2 2.4 copy-start.3
  488.2 2.8 copy-start.14
  496.0 2.7 copy-start.47
  504.5 108.0 %collective-permute-start.9 = (bf16[64,64,16]{1,2,0:T(8,128)(2,1)}, bf16[64,64,16]{1,2,0:T(8,128)(2,1)}, u32[]{:S(2)}, u32[]{:S(2)}) collective-permute-start(bf16[64,64,16]{1,2,0:T(8,128)(2,1)} %copy.276), channel_id=1, source_target_pairs={{16,0},{32,16},{48,32},{64,48},{80,64},{96,80},{112,96},{17,1},{33... | collective-permute-start | bytes 393224 | tf_op jit(solution)/shard_map/ppermute | solution.py:18
  505.8 103.3 %collective-permute-start.8 = (bf16[64,64,16]{1,2,0:T(8,128)(2,1)}, bf16[64,64,16]{1,2,0:T(8,128)(2,1)}, u32[]{:S(2)}, u32[]{:S(2)}) collective-permute-start(bf16[64,64,16]{1,2,0:T(8,128)(2,1)} %copy.275), channel_id=1, source_target_pairs={{0,16},{16,32},{32,48},{48,64},{64,80},{80,96},{96,112},{1,17},{17... | collective-permute-start | bytes 393224 | tf_op jit(solution)/shard_map/ppermute | solution.py:15
  522.5 355.0 %all-to-all-start = ((f32[16,64,296]{2,1,0:T(8,128)}), f32[16,64,296]{2,1,0:T(8,128)}, u32[]{:S(2)}, u32[]{:S(2)}) async-start(f32[16,64,296]{2,1,0:T(8,128)} %copy.260), calls=%async_computation | async-start | bytes 3145728 | tf_op jit(solution)/shard_map/all_to_all | solution.py:168
  532.4 330.1 %all-reduce.8.cloned.1.call-start = ((), (), s32[]{:S(2)}) async-start(), calls=%async_computation.6 | async-start | bytes 1179648 | tf_op jit(solution)/shard_map/psum | solution.py:244
  615.9 7.4 copy-start.23
  615.9 7.4 copy-start.24
  617.8 9.1 collective-permute-start.11
  620.8 13.4 %collective-permute-start.10 = (bf16[64,16,160]{2,0,1:T(8,128)(2,1)S(1)}, bf16[64,16,160]{2,0,1:T(8,128)(2,1)S(1)}, u32[]{:S(2)}, u32[]{:S(2)}) collective-permute-start(bf16[64,16,160]{2,0,1:T(8,128)(2,1)S(1)} %get-tuple-element.63), channel_id=1, source_target_pairs={{1,0},{2,1},{3,2},{4,3},{5,4},{6,5},{7,6},{8,7},{9,8},{10,9},{11,1... | collective-permute-start | bytes 983048 | tf_op jit(solution)/shard_map/ppermute | solution.py:18
  685.8 2.7 copy-start.32
  702.4 12.3 %collective-permute-start.13 = (bf16[64,64,16]{1,2,0:T(8,128)(2,1)}, bf16[64,64,16]{1,2,0:T(8,128)(2,1)}, u32[]{:S(2)}, u32[]{:S(2)}) collective-permute-start(bf16[64,64,16]{1,2,0:T(8,128)(2,1)} %copy.292), channel_id=1, source_target_pairs={{16,0},{32,16},{48,32},{64,48},{80,64},{96,80},{112,96},{17,1},{33... | collective-permute-start | bytes 393224 | tf_op jit(solution)/shard_map/ppermute | solution.py:18
  703.7 7.6 collective-permute-start.12
  718.0 17.2 %copy-start.21 = (bf16[64,64,16]{2,0,1:T(8,128)(2,1)S(1)}, bf16[64,64,16]{2,0,1:T(8,128)(2,1)}, u32[]{:S(2)}) copy-start(bf16[64,64,16]{2,0,1:T(8,128)(2,1)} %copy.293) | copy-start | bytes 393220
  718.0 17.3 %copy-start.22 = (bf16[64,64,16]{2,0,1:T(8,128)(2,1)S(1)}, bf16[64,64,16]{2,0,1:T(8,128)(2,1)}, u32[]{:S(2)}) copy-start(bf16[64,64,16]{2,0,1:T(8,128)(2,1)} %copy.294) | copy-start | bytes 393220
  720.9 145.0 %collective-permute-start.15 = (bf16[64,16,160]{2,0,1:T(8,128)(2,1)}, bf16[64,16,160]{2,0,1:T(8,128)(2,1)}, u32[]{:S(2)}, u32[]{:S(2)}) collective-permute-start(bf16[64,16,160]{2,0,1:T(8,128)(2,1)} %get-tuple-element.58), channel_id=1, source_target_pairs={{0,1},{1,2},{2,3},{3,4},{4,5},{5,6},{6,7},{7,8},{8,9},{9,10},{10,1... | collective-permute-start | bytes 983048 | tf_op jit(solution)/shard_map/ppermute | solution.py:15
  729.4 136.5 %collective-permute-start.14 = (bf16[64,16,160]{2,0,1:T(8,128)(2,1)}, bf16[64,16,160]{2,0,1:T(8,128)(2,1)}, u32[]{:S(2)}, u32[]{:S(2)}) collective-permute-start(bf16[64,16,160]{2,0,1:T(8,128)(2,1)} %get-tuple-element.59), channel_id=1, source_target_pairs={{1,0},{2,1},{3,2},{4,3},{5,4},{6,5},{7,6},{8,7},{9,8},{10,9},{11,1... | collective-permute-start | bytes 983048 | tf_op jit(solution)/shard_map/ppermute | solution.py:18
  873.2 2.5 copy-start.39
  881.7 31.2 %all-to-all-start.1 = ((f32[1024,1,296]{2,1,0:T(1,128)}), f32[1024,1,296]{2,1,0:T(1,128)}, u32[]{:S(2)}, u32[]{:S(2)}) async-start(f32[1024,1,296]{2,1,0:T(1,128)} %copy.261), calls=%async_computation.1 | async-start | bytes 3145728 | tf_op jit(solution)/shard_map/all_to_all | solution.py:175
  888.8 2.5 copy-start.42
  915.8 27.1 %all-to-all-start.2 = ((f32[8,16,8,296]{3,2,0,1:T(8,128)}), f32[8,16,8,296]{3,2,0,1:T(8,128)}, u32[]{:S(2)}, u32[]{:S(2)}) async-start(f32[8,16,8,296]{3,2,0,1:T(8,128)} %copy.263), calls=%async_computation.2 | async-start | bytes 3145728 | tf_op jit(solution)/shard_map/all_to_all | solution.py:182
  955.1 11.2 %copy-start.37 = (f32[5,8,64,128]{3,2,1,0:T(8,128)S(1)}, f32[5,8,64,128]{3,2,1,0:T(8,128)}, u32[]{:S(2)}) copy-start(f32[5,8,64,128]{3,2,1,0:T(8,128)} %copy.361) | copy-start | bytes 3932164
  955.1 12.2 %copy-start.1 = (bf16[37,64]{1,0:T(8,128)(2,1)S(1)}, bf16[37,64]{1,0:T(8,128)(2,1)}, u32[]{:S(2)}) copy-start(bf16[37,64]{1,0:T(8,128)(2,1)} %param.9) | copy-start | bytes 14212
  (25 other events, 36.6 us)
Sparse Core Ops, SparseCore 0:
  711.4 151.1 all-reduce.7
